TPU v7x, 128 devices: a whole 4x4x4 slice. The times are simulated.
128 devices in a mesh: sx: 8 (over z, core), sy: 16 (over y, x).
Axes of the slice: x: 4, y: 4, z: 4, core: 2. Of those that a mesh axis runs over, the one named last changes fastest.
Arguments:
- grid_points: float32 [3, 262144], P(None, ('sx', 'sy')), may hold values from 0 to 16
- weighted_density: float32 [262144], P(('sx', 'sy')), may hold values from -0.15 to 0.15
- point_slot: int32 [262144], P(('sx', 'sy')), may hold values from 0 to 127, as said below
- near_slot: int32 [2048, 64], P(('sx', 'sy')), may hold values from 0 to 127, as said below
- slot_atom: int32 [16384], replicated, may hold values from 0 to 2047, as said below
- atom_pos: float32 [3, 2048], replicated, may hold values from 0 to 16
- decay_rates: float32 [128], replicated, may hold values from 0.5 to 2
- green: float32 [7, 128, 128], replicated, may hold values from -0.5 to 0.5
- moment_table: float32 [3, 128], replicated, may hold values from 0.5 to 5
Outputs:
- potential: float32 [262144], P(('sx', 'sy'))
Inputs may be any that keep to these rules, and one draw needn't show every extreme that they name: `slot_atom`: atoms are owned in ranges in device order: devices below 32 own 2 * 16 atoms each, those below 64 own 16, the rest 16 // 2; the 128 atoms listed by one device are distinct; at most 2 of them have one owner, and in every draw one owner has exactly 2 atoms in every device's list. `near_slot`: the 64 entries of one batch are distinct. `point_slot`: each point's entry is one of its batch's near entries.
All inputs are finite; a program needn't handle non-finite values.
Results may differ from a plain program's by a relative error of at most 0.004.
Values may be sent and summed in bfloat16 or wider, within the bound.
A program may use at most 64 MiB of HBM per device.

v0:
```python
import math
import jax
import jax.numpy as jnp
import numpy as np
from jax import lax
from jax.sharding import PartitionSpec as P

HARM = 49
NRAD = 128
OWN_AVG = 16
OWN = 32


def harmonic_table(comp_x, comp_y, comp_z, top_degree):
    square = comp_x * comp_x + comp_y * comp_y + comp_z * comp_z
    cosines = [jnp.ones_like(comp_x)]
    sine_terms = [jnp.zeros_like(comp_x)]
    for m in range(1, top_degree + 1):
        cosines.append(cosines[m - 1] * comp_x - sine_terms[m - 1] * comp_y)
        sine_terms.append(cosines[m - 1] * comp_y + sine_terms[m - 1] * comp_x)
    legendre = {}
    for m in range(top_degree + 1):
        legendre[m, m] = float(math.prod(range(1, 2 * m, 2))) * cosines[0]
        if m + 1 <= top_degree:
            legendre[m + 1, m] = (2 * m + 1) * comp_z * legendre[m, m]
        for l in range(m + 2, top_degree + 1):
            legendre[l, m] = (
                (2 * l - 1) * comp_z * legendre[l - 1, m]
                - (l + m - 1) * square * legendre[l - 2, m]
            ) / (l - m)
    stacked = []
    for l in range(top_degree + 1):
        for m in range(l + 1):
            factor = math.sqrt(
                (2 * l + 1) / (4 * math.pi) * math.factorial(l - m) / math.factorial(l + m)
            )
            if m == 0:
                stacked.append(factor * legendre[l, 0])
            else:
                factor = factor * math.sqrt(2.0)
                stacked.append(factor * legendre[l, m] * cosines[m])
                stacked.append(factor * legendre[l, m] * sine_terms[m])
    return jnp.stack(stacked)


def soft_geometry(delta):
    distance = jnp.sqrt(jnp.sum(delta * delta, axis=0) + 1.0)
    return (distance, delta / distance)


def shell_layout(decay_rates):
    count = decay_rates.shape[0]
    spacing = 27.0 / (count - 1)
    centres = 1.0 + spacing * jnp.arange(count).astype(decay_rates.dtype)
    return (centres, spacing)


def shell_values(distance, rates, centres, spacing):
    offset = (distance - centres) / spacing
    return jnp.exp(-rates * offset * offset)


def project_points(points, density, slot_of_point, atom_list, atom_pos, decay_rates):
    listed = atom_list.shape[0]
    atom_ids = atom_list[slot_of_point]
    delta = points - atom_pos[:, atom_ids]
    distance, unit_vec = soft_geometry(delta)
    harmonics = harmonic_table(unit_vec[0], unit_vec[1], unit_vec[2], 6)
    projected = (density[None, :] * harmonics).astype(jnp.bfloat16)
    centres, spacing = shell_layout(decay_rates)
    radial = shell_values(
        distance[None, :], decay_rates[:, None], centres[:, None], spacing
    ).astype(jnp.bfloat16)
    onehot = (slot_of_point[None, :] == jnp.arange(listed)[:, None]).astype(jnp.bfloat16)
    weighted = onehot[:, None, :] * projected[None, :, :]
    terms = jnp.einsum("tip,kp->tik", weighted, radial, preferred_element_type=jnp.float32)
    return terms.reshape(listed, -1)


def apply_green(coefficients, green):
    pieces = []
    for l in range(7):
        pieces.append(
            jnp.einsum(
                "aik,kn->ain",
                coefficients[:, l * l : (l + 1) * (l + 1)],
                green[l],
                precision=lax.Precision.HIGHEST,
            )
        )
    return jnp.concatenate(pieces, axis=1)


def low_moments(coefficients, moment_table):
    degrees = np.array([0, 1, 1, 1, 2, 2, 2, 2, 2])
    table = moment_table[degrees]
    return jnp.einsum("aik,ik->ia", coefficients[:, :9], table, precision=lax.Precision.HIGHEST)


def near_field(points, near_ids, near_coef, atom_pos, decay_rates):
    batches = near_ids.shape[0]
    batch_pts = points.shape[1] // batches
    grouped = points.reshape(3, batches, batch_pts)
    delta = grouped[:, :, None, :] - atom_pos[:, near_ids][..., None]
    distance, unit_vec = soft_geometry(delta)
    harmonics = harmonic_table(unit_vec[0], unit_vec[1], unit_vec[2], 6)
    centres, spacing = shell_layout(decay_rates)
    radial = shell_values(
        distance[:, :, None, :],
        decay_rates[None, None, :, None],
        centres[None, None, :, None],
        spacing,
    ).astype(jnp.bfloat16)
    values = jnp.einsum("bjik,bjkp->bjip", near_coef, radial, preferred_element_type=jnp.float32)
    return jnp.sum(values * jnp.moveaxis(harmonics, 0, 2), axis=(1, 2)).reshape(-1)


def far_field(points, near_ids, moments, atom_pos):
    batches = near_ids.shape[0]
    batch_pts = points.shape[1] // batches
    grouped = jnp.moveaxis(points.reshape(3, batches, batch_pts), 1, 0)
    atom_index = jnp.arange(atom_pos.shape[1])

    def one_batch(inputs):
        coords, ids = inputs
        delta = coords[:, :, None] - atom_pos[:, None, :]
        distance, unit_vec = soft_geometry(delta)
        harmonics = harmonic_table(unit_vec[0], unit_vec[1], unit_vec[2], 2)
        inverse = 1.0 / distance
        keep = 1.0 - jnp.sum((ids[:, None] == atom_index[None, :]).astype(jnp.float32), axis=0)
        scaled = moments * keep[None, :]
        total = harmonics[0] * scaled[0][None, :] * inverse
        total = total + jnp.sum(harmonics[1:4] * scaled[1:4, None, :], axis=0) * inverse * inverse
        total = (
            total
            + jnp.sum(harmonics[4:9] * scaled[4:9, None, :], axis=0) * inverse * inverse * inverse
        )
        return jnp.sum(total, axis=1)

    return lax.map(one_batch, (grouped, near_ids)).reshape(-1)


def per_device(
    grid_points,
    weighted_density,
    point_slot,
    near_slot,
    slot_atom,
    atom_pos,
    decay_rates,
    green,
    moment_table,
):
    count_x = lax.axis_size("sx")
    count_y = lax.axis_size("sy")
    devices = count_x * count_y
    myself = lax.axis_index("sx") * count_y + lax.axis_index("sy")
    all_lists = slot_atom.reshape(devices, -1)
    listed = all_lists.shape[1]
    capacity = 2 * listed // devices
    total_atoms = atom_pos.shape[1]
    my_list = all_lists[myself]
    batches = near_slot.shape[0]
    near_count = near_slot.shape[1]
    batch_pts = grid_points.shape[1] // batches
    block = math.gcd(batches, 4)
    groups = batches // block
    group_points = jnp.moveaxis(grid_points.reshape(3, groups, block * batch_pts), 1, 0)
    group_density = weighted_density.reshape(groups, block * batch_pts)
    group_slots = point_slot.reshape(groups, block * batch_pts)
    group_near = near_slot.reshape(groups, block, near_count)
    width = HARM * NRAD

    def project_step(total, inputs):
        points, density, slot_of_point = inputs
        return (
            total + project_points(points, density, slot_of_point, my_list, atom_pos, decay_rates),
            None,
        )

    summed, unused = lax.scan(
        project_step,
        jnp.zeros((listed, width), jnp.float32),
        (group_points, group_density, group_slots),
    )
    partial_value = summed.astype(jnp.bfloat16)
    owner_ids = jnp.arange(devices)
    counts = jnp.where(
        owner_ids < devices // 4,
        2 * OWN_AVG,
        jnp.where(owner_ids < devices // 2, OWN_AVG, OWN_AVG // 2),
    ).astype(jnp.int32)
    range_ends = jnp.cumsum(counts)
    starts = range_ends - counts
    atom_index = jnp.arange(total_atoms)
    owner = jnp.sum((range_ends[None, :] <= atom_index[:, None]).astype(jnp.int32), axis=1)
    owners_all = owner[all_lists]
    my_dest = owners_all[myself]
    slot_index = jnp.arange(listed)
    same_owner = (my_dest[:, None] == my_dest[None, :]) & (
        slot_index[None, :] < slot_index[:, None]
    )
    earlier = jnp.sum(same_owner.astype(jnp.int32), axis=1)
    send_row = my_dest * capacity + earlier
    packing = (jnp.arange(devices * capacity)[:, None] == send_row[None, :]).astype(jnp.bfloat16)
    outgoing = jnp.dot(packing, partial_value, preferred_element_type=jnp.float32).astype(
        jnp.bfloat16
    )
    mine = owners_all == myself
    recv_rank = jnp.cumsum(mine.astype(jnp.int32), axis=1) - 1
    target = jnp.where(mine, owner_ids[:, None] * capacity + recv_rank, devices * capacity)
    local_ids = jnp.where(mine, all_lists - starts[myself], OWN)
    row_owned = (
        jnp.full((devices * capacity + 1,), OWN, jnp.int32)
        .at[target.reshape(-1)]
        .set(local_ids.reshape(-1))[: devices * capacity]
    )
    incoming = lax.all_to_all(outgoing, ("sx", "sy"), split_axis=0, concat_axis=0, tiled=True)
    selector = (row_owned[None, :] == jnp.arange(OWN)[:, None]).astype(jnp.bfloat16)
    coeff_own = jnp.dot(selector, incoming, preferred_element_type=jnp.float32).reshape(
        OWN, HARM, NRAD
    )
    pot_own = apply_green(coeff_own, green).astype(jnp.bfloat16).reshape(OWN, width)
    moments_own = low_moments(coeff_own, moment_table)
    reply = jnp.dot(selector.T, pot_own, preferred_element_type=jnp.float32).astype(jnp.bfloat16)
    returned = lax.all_to_all(reply, ("sx", "sy"), split_axis=0, concat_axis=0, tiled=True)
    gathered = lax.all_gather(moments_own, ("sx", "sy"), axis=1, tiled=True)
    column = owner * OWN + atom_index - starts[owner]
    moments_all = gathered[:, column]
    slot_pot = jnp.dot(packing.T, returned, preferred_element_type=jnp.float32).astype(jnp.bfloat16)
    near_ids = my_list[near_slot]
    group_ids = near_ids.reshape(groups, block, near_count)
    list_index = jnp.arange(listed)

    def near_group(inputs):
        points, ids, near_list = inputs
        picker = (near_list[:, :, None] == list_index[None, None, :]).astype(jnp.bfloat16)
        near_coef = jnp.einsum(
            "bjt,tw->bjw", picker, slot_pot, preferred_element_type=jnp.float32
        ).astype(jnp.bfloat16)
        near_coef = near_coef.reshape(block, near_count, HARM, NRAD)
        return near_field(points, ids, near_coef, atom_pos, decay_rates)

    near_part = lax.map(near_group, (group_points, group_ids, group_near)).reshape(-1)
    far_part = far_field(grid_points, near_ids, moments_all, atom_pos)
    return near_part + far_part


def solution(mesh):
    return jax.shard_map(
        per_device,
        mesh=mesh,
        in_specs=(
            P(None, ("sx", "sy")),
            P(("sx", "sy")),
            P(("sx", "sy")),
            P(("sx", "sy"), None),
            P(),
            P(),
            P(),
            P(),
            P(),
        ),
        out_specs=P(("sx", "sy")),
        check_vma=False,
    )
```

profile of v0, /device:TPU:0, one launch (start us, length us, event | category | flops | bytes accessed | tf_op | source)
XLA Modules:
  0.0 600.6 jit_solution(10263275687308145965)
XLA Ops:
  1.6 90.5 %gather_fusion.3 = s32[16384]{0:T(1024)S(1)} fusion(s32[2048]{0:T(1024)S(1)} %convert_reduce_fusion.1, s32[16384]{0:T(1024)S(1)} %fusion.58), kind=kCustom, calls=%fused_computation.3 | custom fusion | bytes 196608 | tf_op jit(solution)/shard_map/gather | solution.py:197
  96.2 83.5 %while.47 = (s32[]{:T(128)}, f32[128,6272]{0,1:T(8,128)S(1)}, s32[4,512]{1,0:T(4,128)S(1)}, f32[4,512]{1,0:T(4,128)}, f32[4,3,512]{2,1,0:T(4,128)}, /*index=5*/s...) while((s32[]{:T(128)}, f32[128,6272]{0,1:T(8,128)S(1)}, ...), condition=%wide.region_7.8_spmd.clone, body=%wide.region_5.7_spmd.clone.sunk | while | flops 827510272 | bytes 13908703 | solution.py:181
  96.8 3.3 gather_fusion.1
  105.4 2.9 stack.25
  109.7 4.5 fusion.142
  114.3 2.7 bitcast_add_fusion.4
  117.6 3.3 gather_fusion.1
  126.3 2.9 stack.25
  130.6 4.5 fusion.142
  135.1 2.7 bitcast_add_fusion.4
  138.5 3.3 gather_fusion.1
  147.1 2.9 stack.25
  151.4 4.5 fusion.142
  156.0 2.7 bitcast_add_fusion.4
  159.4 3.3 gather_fusion.1
  168.0 2.9 stack.25
  172.3 4.5 fusion.142
  176.9 2.7 bitcast_add_fusion.4
  179.6 3.3 convolution_convert_fusion.2
  183.0 7.2 %all_to_all.16 = bf16[128,2,6272]{2,1,0:T(2,128)(2,1)} reshape(bf16[256,6272]{1,0:T(8,128)(2,1)} %convolution_convert_fusion.2) | data formatting | bytes 6422528 | tf_op jit(solution)/shard_map/all_to_all | solution.py:218
  190.1 11.6 %all-to-all-start = ((bf16[128,2,6272]{2,1,0:T(2,128)(2,1)}), bf16[128,2,6272]{2,1,0:T(2,128)(2,1)}, u32[]{:S(2)}, u32[]{:S(2)}) async-start(bf16[128,2,6272]{2,1,0:T(2,128)(2,1)} %all_to_all.16), calls=%async_computation | async-start | bytes 6422528 | tf_op jit(solution)/shard_map/all_to_all | solution.py:218
  202.5 6.6 %gather_fusion.4 = s32[1024]{0:T(1024)S(1)} fusion(s32[128]{0:T(128)S(1)} %get-tuple-element.1387, s32[1024]{0:T(1024)S(1)} %get-tuple-element.976), kind=kCustom, calls=%fused_computation.4 | custom fusion | bytes 12288 | tf_op jit(solution)/shard_map/gather | solution.py:231
  210.5 60.5 %scatter_custom_fusion = s32[257]{0:T(512)S(1)} fusion(s32[16384]{0:T(1024)S(1)} %bitcast.236, s32[16384]{0:T(1024)S(1)} %subtract_select_fusion, s32[]{:T(128)} %constant.1003.clone.1), kind=kCustom, calls=%fused_computation.317 | custom fusion | bytes 1032 | tf_op jit(solution)/shard_map/scatter | solution.py:216
  271.0 12.6 %gather_fusion.6 = s32[2048]{0:T(1024)S(1)} fusion(s32[128]{0:T(128)S(1)} %fusion.85, s32[2048]{0:T(1024)S(1)} %broadcast_clamp_fusion.1), kind=kCustom, calls=%fused_computation.6 | custom fusion | bytes 24576 | tf_op jit(solution)/shard_map/gather | solution.py:228
  284.3 6.3 %all_to_all.18 = bf16[256,6272]{1,0:T(8,128)(2,1)S(1)} reshape(bf16[128,2,6272]{2,1,0:T(2,128)(2,1)} %all-to-all-done) | data formatting | bytes 6422528 | tf_op jit(solution)/shard_map/all_to_all | solution.py:218
  290.5 3.5 copy.274
  294.0 2.9 fusion.77
  305.8 2.8 all_to_all.19
  308.6 9.7 %all-to-all-start.1 = ((bf16[128,2,6272]{2,1,0:T(2,128)(2,1)}), bf16[128,2,6272]{2,1,0:T(2,128)(2,1)S(1)}, u32[]{:S(2)}, u32[]{:S(2)}) async-start(bf16[128,2,6272]{2,1,0:T(2,128)(2,1)} %all_to_all.19), calls=%async_computation.1 | async-start | bytes 6422528 | tf_op jit(solution)/shard_map/all_to_all | solution.py:226
  319.5 94.5 %all-gather = f32[128,32,9]{1,2,0:T(8,128)} all-gather(f32[1,32,9]{1,2,0:T(8,128)S(1)} %bitcast.239), channel_id=1, replica_groups=mesh['sx'=8,'sy'=16] {'sx','sy'}, dimensions={0}, use_global_device_ids=true | all-gather | bytes 148608 | tf_op jit(solution)/shard_map/all_gather | solution.py:227
  414.0 3.4 copy.277
  417.4 9.2 %gather_fusion.7 = f32[2048,9]{1,0:T(8,128)} fusion(f32[9,4096]{0,1:T(8,128)} %bitcast.216, s32[2048]{0:T(1024)S(1)} %broadcast_clamp_fusion), kind=kCustom, calls=%fused_computation.7 | custom fusion | bytes 155648 | tf_op jit(solution)/shard_map/gather | solution.py:229
  428.1 72.1 %while.46 = (s32[]{:T(128)}, f32[16,128]{1,0:T(8,128)S(1)}, f32[16,3,128]{2,1,0:T(4,128)S(1)}, f32[3,2048]{1,0:T(4,128)S(1)}, s32[16,64]{1,0:T(8,128)S(1)}, /*index=5*/f32[9,2048]{1,0:T(8,128)S(1)}, s32[]{:T(128)}, s32[]{:T(128)}) while((s32[]{:T(128)}, f32[16,128]{1,0:T(8,128)S(1)}, f32[16,3,128]{2,1,0:T(4,128)S(1)}, ...), condition=%wide.region_18.19_spmd.clone, body=%wide.region_12.18_spmd.clone.sunk | while | flops 21122944 | bytes 44499296 | solution.py:140
  500.2 2.8 all_to_all.21
  503.0 3.7 convolution_convert_fusion.3
  506.7 93.2 %while.45 = (s32[]{:T(128)}, f32[4,512]{1,0:T(4,128)S(1)}, s32[4,4,64]{2,1,0:T(4,128)S(1)}, bf16[128,6272]{1,0:T(8,128)(2,1)}, f32[4,3,512]{2,1,0:T(4,128)S(1)},...) while((s32[]{:T(128)}, f32[4,512]{1,0:T(4,128)S(1)}, ...), condition=%wide.region_11.12_spmd.clone, body=%wide.region_8.11_spmd.clone.sunk | while | flops 861898496 | bytes 92647080 | solution.py:244
  515.7 3.1 reshape.986
  518.7 6.9 %fusion.129 = f32[4,64,49,128]{3,2,1,0:T(8,128)S(1)} fusion(bf16[4,64,49,128]{3,2,1,0:T(8,128)(2,1)} %reshape.986, f32[128]{0:T(128)S(1)} %multiply_bitcast_fusion.4, f32[128]{0:T(128)S(1)} %multiply_add_fusion.29, f32[4,64,128]{2,1,0:T(8,128)S(1)} %add_sqrt_fusion.6), kind=kOutput, calls=%fused_computation.17.clone.1 | convolution fusion | flops 432013312 | bytes 9765888 | tf_op jit(solution)/shard_map/while/body/eval_jaxpr/bjik,bjkp->bjip/dot_general | solution.py:114
  525.7 4.3 fusion.130
  539.0 3.1 reshape.986
  542.0 6.9 %fusion.129 = f32[4,64,49,128]{3,2,1,0:T(8,128)S(1)} fusion(bf16[4,64,49,128]{3,2,1,0:T(8,128)(2,1)} %reshape.986, f32[128]{0:T(128)S(1)} %multiply_bitcast_fusion.4, f32[128]{0:T(128)S(1)} %multiply_add_fusion.29, f32[4,64,128]{2,1,0:T(8,128)S(1)} %add_sqrt_fusion.6), kind=kOutput, calls=%fused_computation.17.clone.1 | convolution fusion | flops 432013312 | bytes 9765888 | tf_op jit(solution)/shard_map/while/body/eval_jaxpr/bjik,bjkp->bjip/dot_general | solution.py:114
  549.0 4.3 fusion.130
  562.3 3.1 reshape.986
  565.4 6.9 %fusion.129 = f32[4,64,49,128]{3,2,1,0:T(8,128)S(1)} fusion(bf16[4,64,49,128]{3,2,1,0:T(8,128)(2,1)} %reshape.986, f32[128]{0:T(128)S(1)} %multiply_bitcast_fusion.4, f32[128]{0:T(128)S(1)} %multiply_add_fusion.29, f32[4,64,128]{2,1,0:T(8,128)S(1)} %add_sqrt_fusion.6), kind=kOutput, calls=%fused_computation.17.clone.1 | convolution fusion | flops 432013312 | bytes 9765888 | tf_op jit(solution)/shard_map/while/body/eval_jaxpr/bjik,bjkp->bjip/dot_general | solution.py:114
  572.3 4.3 fusion.130
  585.6 3.1 reshape.986
  588.7 6.9 %fusion.129 = f32[4,64,49,128]{3,2,1,0:T(8,128)S(1)} fusion(bf16[4,64,49,128]{3,2,1,0:T(8,128)(2,1)} %reshape.986, f32[128]{0:T(128)S(1)} %multiply_bitcast_fusion.4, f32[128]{0:T(128)S(1)} %multiply_add_fusion.29, f32[4,64,128]{2,1,0:T(8,128)S(1)} %add_sqrt_fusion.6), kind=kOutput, calls=%fused_computation.17.clone.1 | convolution fusion | flops 432013312 | bytes 9765888 | tf_op jit(solution)/shard_map/while/body/eval_jaxpr/bjik,bjkp->bjip/dot_general | solution.py:114
  595.6 4.3 fusion.130
  (802 shorter events, 153.0 us)
Async XLA Ops:
  0.0 283.6 %copy-start = (f32[3,128]{1,0:T(4,128)S(1)}, f32[3,128]{1,0:T(4,128)}, u32[]{:S(2)}) copy-start(f32[3,128]{1,0:T(4,128)} %param.25) | copy-start | bytes 4612
  0.3 91.8 %copy-start.17 = (s32[128]{0:T(128)}, s32[128]{0:T(128)S(1)}, u32[]{:S(2)}) copy-start(s32[128]{0:T(128)S(1)} %reduce) | copy-start | bytes 1540
  1.5 90.8 %copy-start.5 = (f32[3,2048]{1,0:T(4,128)S(1)}, f32[3,2048]{1,0:T(4,128)}, u32[]{:S(2)}) copy-start(f32[3,2048]{1,0:T(4,128)} %param.22) | copy-start | bytes 73732
  1.5 92.2 %copy-start.20 = (f32[128]{0:T(128)S(1)}, f32[128]{0:T(128)}, u32[]{:S(2)}) copy-start(f32[128]{0:T(128)} %param.23) | copy-start | bytes 1540
  1.5 92.8 %copy-start.14 = (s32[2048]{0:T(1024)S(1)}, s32[2048]{0:T(1024)}, u32[]{:S(2)}) copy-start(s32[2048]{0:T(1024)} %param.19) | copy-start | bytes 24580
  1.6 92.8 %copy-start.15 = (f32[2048]{0:T(1024)S(1)}, f32[2048]{0:T(1024)}, u32[]{:S(2)}) copy-start(f32[2048]{0:T(1024)} %param.18) | copy-start | bytes 24580
  92.1 4.0 copy-start.8
  96.2 0.6 copy-start.12
  103.3 0.6 copy-start.10
  114.3 2.8 copy-start.13
  117.0 0.6 copy-start.12
  124.1 0.6 copy-start.10
  135.1 2.8 copy-start.13
  137.9 0.6 copy-start.12
  145.0 0.6 copy-start.10
  156.0 2.8 copy-start.13
  158.8 0.6 copy-start.12
  165.9 0.6 copy-start.10
  176.9 2.8 copy-start.13
  183.0 18.8 %copy-start.9 = (s32[16384]{0:T(1024)S(1)}, s32[16384]{0:T(1024)}, u32[]{:S(2)}) copy-start(s32[16384]{0:T(1024)} %copy-done.8) | copy-start | bytes 196612
  183.0 19.4 %copy-start.11 = (s32[16,64]{1,0:T(8,128)S(1)}, s32[16,64]{1,0:T(8,128)}, u32[]{:S(2)}) copy-start(s32[16,64]{1,0:T(8,128)} %param.20) | copy-start | bytes 12292
  183.0 19.5 %copy-start.19 = (s32[9]{0:T(128)S(1)}, s32[9]{0:T(128)}, u32[]{:S(2)}) copy-start(s32[9]{0:T(128)} %constant.1017) | copy-start | bytes 112
  190.1 19.1 %copy-start.18 = (s32[128]{0:T(128)S(1)}, s32[128]{0:T(128)}, u32[]{:S(2)}) copy-start(s32[128]{0:T(128)} %copy-done.17) | copy-start | bytes 1540
  190.1 19.7 %copy-start.7 = (s32[16384]{0:T(1024)S(1)}, s32[16384]{0:T(1024)}, u32[]{:S(2)}) copy-start(s32[16384]{0:T(1024)} %param.21) | copy-start | bytes 196612
  190.1 94.1 %all-to-all-start = ((bf16[128,2,6272]{2,1,0:T(2,128)(2,1)}), bf16[128,2,6272]{2,1,0:T(2,128)(2,1)}, u32[]{:S(2)}, u32[]{:S(2)}) async-start(bf16[128,2,6272]{2,1,0:T(2,128)(2,1)} %all_to_all.16), calls=%async_computation | async-start | bytes 6422528 | tf_op jit(solution)/shard_map/all_to_all | solution.py:218
  296.9 6.6 %copy-start.4 = (f32[32,49,128]{2,0,1:T(8,128)}, f32[32,49,128]{2,0,1:T(8,128)S(1)}, u32[]{:S(2)}) copy-start(f32[32,49,128]{2,0,1:T(8,128)S(1)} %fusion.77) | copy-start | bytes 2408452
  308.6 119.6 %copy-start.6 = (f32[4,3,512]{2,1,0:T(4,128)S(1)}, f32[4,3,512]{2,1,0:T(4,128)}, u32[]{:S(2)}) copy-start(f32[4,3,512]{2,1,0:T(4,128)} %get-tuple-element.1392) | copy-start | bytes 73732
  308.6 191.7 %all-to-all-start.1 = ((bf16[128,2,6272]{2,1,0:T(2,128)(2,1)}), bf16[128,2,6272]{2,1,0:T(2,128)(2,1)S(1)}, u32[]{:S(2)}, u32[]{:S(2)}) async-start(bf16[128,2,6272]{2,1,0:T(2,128)(2,1)} %all_to_all.19), calls=%async_computation.1 | async-start | bytes 6422528 | tf_op jit(solution)/shard_map/all_to_all | solution.py:226
  500.2 2.8 copy-start.16
  500.2 6.5 %copy-start.21 = (f32[1,1,128,1]{2,3,1,0:T(1,128)S(1)}, f32[1,1,128,1]{2,3,1,0:T(1,128)}, u32[]{:S(2)}) copy-start(f32[1,1,128,1]{2,3,1,0:T(1,128)} %get-tuple-element.1340) | copy-start | bytes 1540
  510.3 4.3 copy-start.3
  511.9 2.7 copy-start.2
  533.6 4.3 copy-start.3
  535.2 2.7 copy-start.2
  556.9 4.3 copy-start.3
  558.5 2.7 copy-start.2
  580.2 4.3 copy-start.3
  581.8 2.7 copy-start.2
  599.9 0.7 copy-start.1
where the time goes:
time: 604 us; the launch traced here: 601 us
  local copies, waits for them, and re-layouts  286 us (47%)
  other arithmetic  124 us (21%)
  blocking collectives  94.5 us (16%)
  matrix products  70.1 us (12%)
  starting transfers between devices  21.3 us (4%)
    all_gather x1, blocking collectives, per_device(): gathered = lax.all_gather(moments_own, ('sx', 'sy'), axis=1, tiled=True)  94.5 us
    gather x2, local copies, waits for them, and re-layouts, per_device(): owners_all = owner[all_lists]  90.6 us
    scatter x1, local copies, waits for them, and re-layouts, per_device(): row_owned = jnp.full((devices * capacity + 1,), OWN, jnp.int32).at[target...  60.5 us
    dot_general x4, matrix products, near_field(): jnp.einsum('bjik,bjkp->bjip', near_coef, radial, preferred_element_type=j...  27.8 us
    while x236, other arithmetic  21 us
    dot_general x4, matrix products, project_points(): jnp.einsum('tip,kp->tik', weighted, radial, preferred_element_type=jnp.fl...  18.2 us
    reduce_sum x4, other arithmetic, near_field(): jnp.sum(values * jnp.moveaxis(harmonics, 0, 2), axis=(1, 2)).reshape(-1)  17.1 us
    all_to_all x3, local copies, waits for them, and re-layouts, per_device(): lax.all_to_all(outgoing, ('sx', 'sy'), split_axis=0, concat_axis=0, tiled...  16.9 us
  transfers between devices with their start and end apart: 2, of which 0 were waited for; matrix products, arithmetic and copies ran while one was open for 28% of the time, Pallas kernels for 0%

commit v1 on v0

--- a/solution.py
+++ b/solution.py
@@ -224,7 +224,10 @@
     moments_own = low_moments(coeff_own, moment_table)
     reply = jnp.dot(selector.T, pot_own, preferred_element_type=jnp.float32).astype(jnp.bfloat16)
     returned = lax.all_to_all(reply, ("sx", "sy"), split_axis=0, concat_axis=0, tiled=True)
-    gathered = lax.all_gather(moments_own, ("sx", "sy"), axis=1, tiled=True)
+    gathered = jnp.concatenate(
+        lax.all_to_all(jnp.stack([moments_own] * lax.axis_size(("sx", "sy"))), ("sx", "sy"), 0, 0),
+        axis=1,
+    )
     column = owner * OWN + atom_index - starts[owner]
     moments_all = gathered[:, column]
     slot_pot = jnp.dot(packing.T, returned, preferred_element_type=jnp.float32).astype(jnp.bfloat16)

time: 604 us -> 517 us (0.86)
  blocking collectives: 94.5 us -> 0 us
    all_gather x1 -> x0, blocking collectives: 94.5 us -> none  [per_device(): gathered = lax.all_gather(moments_own, ('sx', 'sy'), axis=1, tiled=True)]
    all_to_all x0 -> x1, starting transfers between devices: none -> 9.69 us  [per_device(): lax.all_to_all(jnp.stack([moments_own] * lax.axis_size(('sx', 'sy'))), ('...]
  transfers between devices with their start and end apart: 2 -> 3, of which waited for: 0 -> 1; matrix products, arithmetic and copies ran while one was open for 28% -> 31% of each run, Pallas kernels for 0% -> 0%
where the time goes in v1:
time: 517 us; the launch traced here: 515 us
  local copies, waits for them, and re-layouts  284 us (55%)
  other arithmetic  124 us (24%)
  matrix products  68.3 us (13%)
  starting transfers between devices  27.3 us (5%)
  waiting for transfers between devices  5.41 us (1%)
    gather x2, local copies, waits for them, and re-layouts, per_device(): owners_all = owner[all_lists]  90.6 us
    scatter x1, local copies, waits for them, and re-layouts, per_device(): row_owned = jnp.full((devices * capacity + 1,), OWN, jnp.int32).at[target...  60.5 us
    dot_general x4, matrix products, near_field(): jnp.einsum('bjik,bjkp->bjip', near_coef, radial, preferred_element_type=j...  27.7 us
    while x236, other arithmetic  21 us
    dot_general x4, matrix products, project_points(): jnp.einsum('tip,kp->tik', weighted, radial, preferred_element_type=jnp.fl...  18.3 us
    reduce_sum x4, other arithmetic, near_field(): jnp.sum(values * jnp.moveaxis(harmonics, 0, 2), axis=(1, 2)).reshape(-1)  17.1 us
    all_to_all x3, local copies, waits for them, and re-layouts, per_device(): lax.all_to_all(outgoing, ('sx', 'sy'), split_axis=0, concat_axis=0, tiled...  16.9 us
    while x44, local copies, waits for them, and re-layouts  15.4 us
  transfers between devices with their start and end apart: 3, of which 1 were waited for; matrix products, arithmetic and copies ran while one was open for 31% of the time, Pallas kernels for 0%

profile of v1, /device:TPU:0, one launch (start us, length us, event | category | flops | bytes accessed | tf_op | source)
XLA Modules:
  0.0 514.5 jit_solution(2953137239152245123)
XLA Ops:
  1.6 90.5 %gather_fusion.3 = s32[16384]{0:T(1024)S(1)} fusion(s32[2048]{0:T(1024)S(1)} %convert_reduce_fusion.1, s32[16384]{0:T(1024)S(1)} %fusion.58), kind=kCustom, calls=%fused_computation.3 | custom fusion | bytes 196608 | tf_op jit(solution)/shard_map/gather | solution.py:197
  96.1 83.7 %while.47 = (s32[]{:T(128)}, f32[128,6272]{0,1:T(8,128)S(1)}, s32[4,512]{1,0:T(4,128)S(1)}, f32[4,512]{1,0:T(4,128)}, f32[4,3,512]{2,1,0:T(4,128)}, /*index=5*/s...) while((s32[]{:T(128)}, f32[128,6272]{0,1:T(8,128)S(1)}, ...), condition=%wide.region_7.8_spmd.clone, body=%wide.region_5.7_spmd.clone.sunk | while | flops 827510272 | bytes 13908703 | solution.py:181
  96.7 3.3 gather_fusion.1
  105.4 2.9 stack.28
  109.7 4.6 fusion.142
  114.3 2.7 bitcast_add_fusion.4
  117.7 3.3 gather_fusion.1
  126.3 2.9 stack.28
  130.6 4.6 fusion.142
  135.2 2.7 bitcast_add_fusion.4
  138.6 3.3 gather_fusion.1
  147.2 2.9 stack.28
  151.6 4.6 fusion.142
  156.1 2.7 bitcast_add_fusion.4
  159.5 3.3 gather_fusion.1
  168.2 2.9 stack.28
  172.5 4.6 fusion.142
  177.1 2.7 bitcast_add_fusion.4
  179.8 3.3 convolution_convert_fusion.2
  183.2 7.2 %all_to_all.19 = bf16[128,2,6272]{2,1,0:T(2,128)(2,1)} reshape(bf16[256,6272]{1,0:T(8,128)(2,1)} %convolution_convert_fusion.2) | data formatting | bytes 6422528 | tf_op jit(solution)/shard_map/all_to_all | solution.py:218
  190.3 11.6 %all-to-all-start = ((bf16[128,2,6272]{2,1,0:T(2,128)(2,1)}), bf16[128,2,6272]{2,1,0:T(2,128)(2,1)}, u32[]{:S(2)}, u32[]{:S(2)}) async-start(bf16[128,2,6272]{2,1,0:T(2,128)(2,1)} %all_to_all.19), calls=%async_computation | async-start | bytes 6422528 | tf_op jit(solution)/shard_map/all_to_all | solution.py:218
  202.7 6.6 %gather_fusion.4 = s32[1024]{0:T(1024)S(1)} fusion(s32[128]{0:T(128)S(1)} %get-tuple-element.1387, s32[1024]{0:T(1024)S(1)} %get-tuple-element.976), kind=kCustom, calls=%fused_computation.4 | custom fusion | bytes 12288 | tf_op jit(solution)/shard_map/gather | solution.py:234
  210.7 60.5 %scatter_custom_fusion = s32[257]{0:T(512)S(1)} fusion(s32[16384]{0:T(1024)S(1)} %bitcast.232, s32[16384]{0:T(1024)S(1)} %subtract_select_fusion, s32[]{:T(128)} %constant.1003.clone.1), kind=kCustom, calls=%fused_computation.317 | custom fusion | bytes 1032 | tf_op jit(solution)/shard_map/scatter | solution.py:216
  271.2 12.6 %gather_fusion.6 = s32[2048]{0:T(1024)S(1)} fusion(s32[128]{0:T(128)S(1)} %fusion.85, s32[2048]{0:T(1024)S(1)} %broadcast_clamp_fusion.1), kind=kCustom, calls=%fused_computation.6 | custom fusion | bytes 24576 | tf_op jit(solution)/shard_map/gather | solution.py:231
  284.5 6.3 %all_to_all.21 = bf16[256,6272]{1,0:T(8,128)(2,1)S(1)} reshape(bf16[128,2,6272]{2,1,0:T(2,128)(2,1)} %all-to-all-done) | data formatting | bytes 6422528 | tf_op jit(solution)/shard_map/all_to_all | solution.py:218
  290.7 3.5 copy.274
  294.2 2.9 fusion.77
  306.9 9.7 %all-to-all-start.2 = ((f32[128,1,288]{2,1,0:T(1,128)}), f32[128,1,288]{2,1,0:T(1,128)S(1)}, u32[]{:S(2)}, u32[]{:S(2)}) async-start(f32[128,1,288]{2,1,0:T(1,128)} %reshape.983), calls=%async_computation.2 | async-start | bytes 393216 | tf_op jit(solution)/shard_map/all_to_all | solution.py:228
  318.6 2.8 all_to_all.22
  321.4 5.4 %all-to-all-done.2 = f32[128,1,288]{2,1,0:T(1,128)S(1)} async-done(((f32[128,1,288]{2,1,0:T(1,128)}), f32[128,1,288]{2,1,0:T(1,128)S(1)}, u32[]{:S(2)}, u32[]{:S(2)}) %all-to-all-start.2) | async-done | bytes 147488 | tf_op jit(solution)/shard_map/all_to_all | solution.py:228
  326.8 6.0 %all-to-all-start.1 = ((bf16[128,2,6272]{2,1,0:T(2,128)(2,1)}), bf16[128,2,6272]{2,1,0:T(2,128)(2,1)}, u32[]{:S(2)}, u32[]{:S(2)}) async-start(bf16[128,2,6272]{2,1,0:T(2,128)(2,1)} %all_to_all.22), calls=%async_computation.1 | async-start | bytes 6422528 | tf_op jit(solution)/shard_map/all_to_all | solution.py:226
  336.4 5.5 %gather_fusion.7 = f32[2048,9]{1,0:T(8,128)S(1)} fusion(f32[9,4096]{0,1:T(8,128)S(1)} %bitcast.211, s32[2048]{0:T(1024)S(1)} %broadcast_clamp_fusion), kind=kCustom, calls=%fused_computation.7 | custom fusion | bytes 155648 | tf_op jit(solution)/shard_map/gather | solution.py:232
  342.2 70.3 %while.46 = (s32[]{:T(128)}, f32[16,128]{1,0:T(8,128)S(1)}, f32[16,3,128]{2,1,0:T(4,128)S(1)}, f32[3,2048]{1,0:T(4,128)S(1)}, s32[16,64]{1,0:T(8,128)S(1)}, /*index=5*/f32[9,2048]{1,0:T(8,128)S(1)}, s32[]{:T(128)}, s32[]{:T(128)}) while((s32[]{:T(128)}, f32[16,128]{1,0:T(8,128)S(1)}, f32[16,3,128]{2,1,0:T(4,128)S(1)}, ...), condition=%wide.region_18.19_spmd.clone, body=%wide.region_12.18_spmd.clone.sunk | while | flops 21122944 | bytes 44499296 | solution.py:140
  412.5 6.3 %all_to_all.24 = bf16[256,6272]{1,0:T(8,128)(2,1)S(1)} reshape(bf16[128,2,6272]{2,1,0:T(2,128)(2,1)} %all-to-all-done.1) | data formatting | bytes 6422528 | tf_op jit(solution)/shard_map/all_to_all | solution.py:226
  420.6 93.2 %while.45 = (s32[]{:T(128)}, f32[4,512]{1,0:T(4,128)S(1)}, s32[4,4,64]{2,1,0:T(4,128)S(1)}, bf16[128,6272]{1,0:T(8,128)(2,1)}, f32[4,3,512]{2,1,0:T(4,128)S(1)},...) while((s32[]{:T(128)}, f32[4,512]{1,0:T(4,128)S(1)}, ...), condition=%wide.region_11.12_spmd.clone, body=%wide.region_8.11_spmd.clone.sunk | while | flops 861898496 | bytes 92647080 | solution.py:247
  425.9 2.7 copy-done.2
  429.6 3.1 reshape.996
  432.7 6.9 %fusion.129 = f32[4,64,49,128]{3,2,1,0:T(8,128)S(1)} fusion(bf16[4,64,49,128]{3,2,1,0:T(8,128)(2,1)} %reshape.996, f32[128]{0:T(128)S(1)} %multiply_bitcast_fusion.4, f32[128]{0:T(128)S(1)} %multiply_add_fusion.29, f32[4,64,128]{2,1,0:T(8,128)S(1)} %add_sqrt_fusion.6), kind=kOutput, calls=%fused_computation.17.clone.1 | convolution fusion | flops 432013312 | bytes 9765888 | tf_op jit(solution)/shard_map/while/body/eval_jaxpr/bjik,bjkp->bjip/dot_general | solution.py:114
  439.6 4.3 fusion.130
  452.9 3.1 reshape.996
  456.0 6.9 %fusion.129 = f32[4,64,49,128]{3,2,1,0:T(8,128)S(1)} fusion(bf16[4,64,49,128]{3,2,1,0:T(8,128)(2,1)} %reshape.996, f32[128]{0:T(128)S(1)} %multiply_bitcast_fusion.4, f32[128]{0:T(128)S(1)} %multiply_add_fusion.29, f32[4,64,128]{2,1,0:T(8,128)S(1)} %add_sqrt_fusion.6), kind=kOutput, calls=%fused_computation.17.clone.1 | convolution fusion | flops 432013312 | bytes 9765888 | tf_op jit(solution)/shard_map/while/body/eval_jaxpr/bjik,bjkp->bjip/dot_general | solution.py:114
  462.9 4.3 fusion.130
  476.2 3.1 reshape.996
  479.3 6.9 %fusion.129 = f32[4,64,49,128]{3,2,1,0:T(8,128)S(1)} fusion(bf16[4,64,49,128]{3,2,1,0:T(8,128)(2,1)} %reshape.996, f32[128]{0:T(128)S(1)} %multiply_bitcast_fusion.4, f32[128]{0:T(128)S(1)} %multiply_add_fusion.29, f32[4,64,128]{2,1,0:T(8,128)S(1)} %add_sqrt_fusion.6), kind=kOutput, calls=%fused_computation.17.clone.1 | convolution fusion | flops 432013312 | bytes 9765888 | tf_op jit(solution)/shard_map/while/body/eval_jaxpr/bjik,bjkp->bjip/dot_general | solution.py:114
  486.2 4.3 fusion.130
  499.5 3.1 reshape.996
  502.6 6.9 %fusion.129 = f32[4,64,49,128]{3,2,1,0:T(8,128)S(1)} fusion(bf16[4,64,49,128]{3,2,1,0:T(8,128)(2,1)} %reshape.996, f32[128]{0:T(128)S(1)} %multiply_bitcast_fusion.4, f32[128]{0:T(128)S(1)} %multiply_add_fusion.29, f32[4,64,128]{2,1,0:T(8,128)S(1)} %add_sqrt_fusion.6), kind=kOutput, calls=%fused_computation.17.clone.1 | convolution fusion | flops 432013312 | bytes 9765888 | tf_op jit(solution)/shard_map/while/body/eval_jaxpr/bjik,bjkp->bjip/dot_general | solution.py:114
  509.5 4.3 fusion.130
  (810 shorter events, 154.6 us)
Async XLA Ops:
  0.0 283.8 %copy-start = (f32[3,128]{1,0:T(4,128)S(1)}, f32[3,128]{1,0:T(4,128)}, u32[]{:S(2)}) copy-start(f32[3,128]{1,0:T(4,128)} %param.25) | copy-start | bytes 4612
  0.3 91.8 %copy-start.18 = (s32[128]{0:T(128)}, s32[128]{0:T(128)S(1)}, u32[]{:S(2)}) copy-start(s32[128]{0:T(128)S(1)} %reduce) | copy-start | bytes 1540
  1.5 90.8 %copy-start.4 = (f32[3,2048]{1,0:T(4,128)S(1)}, f32[3,2048]{1,0:T(4,128)}, u32[]{:S(2)}) copy-start(f32[3,2048]{1,0:T(4,128)} %param.22) | copy-start | bytes 73732
  1.5 92.2 %copy-start.21 = (f32[128]{0:T(128)S(1)}, f32[128]{0:T(128)}, u32[]{:S(2)}) copy-start(f32[128]{0:T(128)} %param.23) | copy-start | bytes 1540
  1.5 92.8 %copy-start.15 = (s32[2048]{0:T(1024)S(1)}, s32[2048]{0:T(1024)}, u32[]{:S(2)}) copy-start(s32[2048]{0:T(1024)} %param.19) | copy-start | bytes 24580
  1.6 92.8 %copy-start.16 = (f32[2048]{0:T(1024)S(1)}, f32[2048]{0:T(1024)}, u32[]{:S(2)}) copy-start(f32[2048]{0:T(1024)} %param.18) | copy-start | bytes 24580
  92.1 4.0 copy-start.9
  96.1 0.6 copy-start.13
  103.2 0.6 copy-start.11
  114.3 2.8 copy-start.14
  117.1 0.6 copy-start.13
  124.2 0.6 copy-start.11
  135.2 2.8 copy-start.14
  138.0 0.6 copy-start.13
  145.1 0.6 copy-start.11
  156.1 2.8 copy-start.14
  158.9 0.6 copy-start.13
  166.0 0.6 copy-start.11
  177.1 2.8 copy-start.14
  183.2 18.8 %copy-start.10 = (s32[16384]{0:T(1024)S(1)}, s32[16384]{0:T(1024)}, u32[]{:S(2)}) copy-start(s32[16384]{0:T(1024)} %copy-done.9) | copy-start | bytes 196612
  183.2 19.4 %copy-start.12 = (s32[16,64]{1,0:T(8,128)S(1)}, s32[16,64]{1,0:T(8,128)}, u32[]{:S(2)}) copy-start(s32[16,64]{1,0:T(8,128)} %param.20) | copy-start | bytes 12292
  183.2 19.5 %copy-start.20 = (s32[9]{0:T(128)S(1)}, s32[9]{0:T(128)}, u32[]{:S(2)}) copy-start(s32[9]{0:T(128)} %constant.1017) | copy-start | bytes 112
  190.3 19.1 %copy-start.19 = (s32[128]{0:T(128)S(1)}, s32[128]{0:T(128)}, u32[]{:S(2)}) copy-start(s32[128]{0:T(128)} %copy-done.18) | copy-start | bytes 1540
  190.3 19.7 %copy-start.8 = (s32[16384]{0:T(1024)S(1)}, s32[16384]{0:T(1024)}, u32[]{:S(2)}) copy-start(s32[16384]{0:T(1024)} %param.21) | copy-start | bytes 196612
  190.3 94.1 %all-to-all-start = ((bf16[128,2,6272]{2,1,0:T(2,128)(2,1)}), bf16[128,2,6272]{2,1,0:T(2,128)(2,1)}, u32[]{:S(2)}, u32[]{:S(2)}) async-start(bf16[128,2,6272]{2,1,0:T(2,128)(2,1)} %all_to_all.19), calls=%async_computation | async-start | bytes 6422528 | tf_op jit(solution)/shard_map/all_to_all | solution.py:218
  304.9 0.7 copy-start.7
  306.9 19.9 %all-to-all-start.2 = ((f32[128,1,288]{2,1,0:T(1,128)}), f32[128,1,288]{2,1,0:T(1,128)S(1)}, u32[]{:S(2)}, u32[]{:S(2)}) async-start(f32[128,1,288]{2,1,0:T(1,128)} %reshape.983), calls=%async_computation.2 | async-start | bytes 393216 | tf_op jit(solution)/shard_map/all_to_all | solution.py:228
  321.4 20.8 %copy-start.6 = (f32[4,3,512]{2,1,0:T(4,128)S(1)}, f32[4,3,512]{2,1,0:T(4,128)}, u32[]{:S(2)}) copy-start(f32[4,3,512]{2,1,0:T(4,128)} %get-tuple-element.1390) | copy-start | bytes 73732
  326.8 6.0 %copy-start.5 = (f32[128,1,288]{2,1,0:T(1,128)}, f32[128,1,288]{2,1,0:T(1,128)S(1)}, u32[]{:S(2)}) copy-start(f32[128,1,288]{2,1,0:T(1,128)S(1)} %all-to-all-done.2) | copy-start | bytes 442372
  326.8 85.7 %all-to-all-start.1 = ((bf16[128,2,6272]{2,1,0:T(2,128)(2,1)}), bf16[128,2,6272]{2,1,0:T(2,128)(2,1)}, u32[]{:S(2)}, u32[]{:S(2)}) async-start(bf16[128,2,6272]{2,1,0:T(2,128)(2,1)} %all_to_all.22), calls=%async_computation.1 | async-start | bytes 6422528 | tf_op jit(solution)/shard_map/all_to_all | solution.py:226
  412.5 6.3 %copy-start.17 = (s32[128]{0:T(128)S(1)}, s32[128]{0:T(128)}, u32[]{:S(2)}) copy-start(s32[128]{0:T(128)} %get-tuple-element.973) | copy-start | bytes 1540
  412.5 8.1 %copy-start.22 = (f32[1,1,128,1]{2,3,1,0:T(1,128)S(1)}, f32[1,1,128,1]{2,3,1,0:T(1,128)}, u32[]{:S(2)}) copy-start(f32[1,1,128,1]{2,3,1,0:T(1,128)} %get-tuple-element.1340) | copy-start | bytes 1540
  424.2 4.3 copy-start.3
  425.8 2.7 copy-start.2
  447.5 4.3 copy-start.3
  449.1 2.7 copy-start.2
  470.8 4.3 copy-start.3
  472.4 2.7 copy-start.2
  494.1 4.3 copy-start.3
  495.7 2.7 copy-start.2
  513.8 0.7 copy-start.1
